TPU v7x, 32 devices: a whole 2x2x4 slice. The times are simulated.
32 devices in a mesh: shot: 2 (over y), box: 8 (over z, x), sub: 2 (over core).
Axes of the slice: x: 2, y: 2, z: 4, core: 2. Of those that a mesh axis runs over, the one named last changes fastest.
Arguments:
- box_weights: float32 [64, 256, 128], P(('shot', 'box', 'sub')), parts along dimension 0, may hold values from -6 to 6
- velocity: float32 [8192], P('shot'), parts along dimension 0, may hold values from -4 to 4
- switch_kernel: float32 [128, 128], replicated, may hold values from -0.5 to 0.5
Outputs:
- final_weights: float32 [4, 4096, 128], P('shot', ('box', 'sub')), parts along dimension 0
There are 2 independent parts, one for each index of `shot`. A program takes and returns all parts, laid end to end along the dimension named above; an argument that names none is the same for every part. Nothing has to cross between parts.
All inputs are finite; a program needn't handle non-finite values.
Results may differ from a plain program's by a relative error of at most 0.00013.
Values sent between devices are 32-bit elements; how exact they have to be, the bound alone decides.
No kernel may reach another device: no remote copies, remote signals or barrier semaphores. Data moves between devices by JAX's collectives and lax.ppermute only.
A program may use at most 64 MiB of HBM per device.

v0:
```python
import jax
import jax.numpy as jnp
from jax import lax
from jax.sharding import PartitionSpec as P

CHEB = 8
half_root = 0.7071067811865476


def swapped(value, axis, apart):
    mask = 2**apart
    pairs = [(source, source ^ mask) for source in range(lax.axis_size(axis))]
    return lax.ppermute(value, axis, pairs)


def cheb_nodes():
    counter = jnp.arange(CHEB, dtype=jnp.float32)
    return jnp.cos(jnp.pi * (2.0 * counter + 1.0) / (2.0 * CHEB))


def lagrange_rows(points, node_values):
    differences = points[:, None] - node_values[None, :]
    node_gaps = node_values[:, None] - node_values[None, :]
    identity = jnp.eye(CHEB, dtype=jnp.float32)
    numerator = jnp.prod(
        jnp.where(identity[None, :, :] > 0.5, 1.0, differences[:, None, :]), axis=2
    )
    denominator = jnp.prod(jnp.where(identity > 0.5, 1.0, node_gaps), axis=1)
    return numerator / denominator[None, :]


def spread_coord(values, axis_dim):
    if axis_dim == 0:
        return jnp.repeat(values, CHEB)
    return jnp.tile(values, CHEB)


def level_tables(axis_dim):
    node_values = cheb_nodes()
    identity = jnp.eye(CHEB, dtype=jnp.float32)
    pair_eye = jnp.eye(2, dtype=jnp.float32)
    matrices = []
    coords = []
    for child_idx in (0, 1):
        child_pts = (node_values + (2.0 * child_idx - 1.0)) * 0.5
        lagrange = lagrange_rows(child_pts, node_values)
        if axis_dim == 0:
            single = jnp.kron(lagrange, identity)
        else:
            single = jnp.kron(identity, lagrange)
        matrices.append(jnp.kron(pair_eye, single))
        coords.append(spread_coord(child_pts, axis_dim))
    return (jnp.concatenate(matrices, 0), jnp.stack(coords), spread_coord(node_values, axis_dim))


def rotate(values, angles):
    real_part = values[..., : CHEB * CHEB]
    imag_part = values[..., CHEB * CHEB :]
    cosines = jnp.cos(angles)
    sine_vals = jnp.sin(angles)
    return jnp.concatenate(
        [real_part * cosines - imag_part * sine_vals, real_part * sine_vals + imag_part * cosines],
        -1,
    )


def merge_blocks(blocks, omegas, weights, coord_in, coord_out):
    phase = omegas[None, None, :, :, None]
    first_term = rotate(blocks[:, 0][:, :, None], -phase * coord_in[0])
    second_term = rotate(blocks[:, 1][:, :, None], -phase * coord_in[1])
    joined = jnp.concatenate([first_term, second_term], -1)
    mixture = jnp.dot(
        joined.reshape(-1, 4 * CHEB * CHEB),
        weights,
        precision=lax.Precision.HIGHEST,
        preferred_element_type=jnp.float32,
    )
    mixture = mixture.reshape(first_term.shape)
    return rotate(mixture, phase * coord_out) * half_root


def apply_switch(current, switch_kernel):
    flat = jnp.dot(
        current.reshape(-1, current.shape[-1]),
        switch_kernel,
        precision=lax.Precision.HIGHEST,
        preferred_element_type=jnp.float32,
    )
    return flat.reshape(current.shape)


def level_omegas(velocity, device, level_idx, tgt_count):
    tgt_code = device % 2 ** (level_idx + 1)
    return lax.dynamic_slice_in_dim(velocity, tgt_code * tgt_count, tgt_count)


def own_part(current, omegas, my_child, level_idx):
    vec_len = current.shape[-1]
    weights, coord_in, coord_out = level_tables(level_idx % 2)
    coord_mine = jnp.where(my_child == 0, coord_in[0], coord_in[1])
    weight_mine = jnp.where(my_child == 0, weights[:vec_len], weights[vec_len:])
    turned = rotate(current, -omegas[None, :, None] * coord_mine[None, None, :])
    return jnp.dot(
        turned.reshape(-1, vec_len),
        weight_mine,
        precision=lax.Precision.HIGHEST,
        preferred_element_type=jnp.float32,
    )


def far_part(own_term, partner, omegas, my_child, level_idx):
    vec_len = partner.shape[-1]
    weights, coord_in, coord_out = level_tables(level_idx % 2)
    coord_other = jnp.where(my_child == 0, coord_in[1], coord_in[0])
    weight_other = jnp.where(my_child == 0, weights[vec_len:], weights[:vec_len])
    turned = rotate(partner, -omegas[None, :, None] * coord_other[None, None, :])
    far_term = jnp.dot(
        turned.reshape(-1, vec_len),
        weight_other,
        precision=lax.Precision.HIGHEST,
        preferred_element_type=jnp.float32,
    )
    mixture = (own_term + far_term).reshape(partner.shape)
    return rotate(mixture, omegas[None, :, None] * coord_out[None, None, :]) * half_root


def body(box_weights, velocity, switch_kernel):
    box_count = lax.axis_size("box")
    sub_count = lax.axis_size("sub")
    box_bits = box_count.bit_length() - 1
    sub_bits = sub_count.bit_length() - 1
    levels = box_bits + sub_bits
    box_index = lax.axis_index("box")
    sub_index = lax.axis_index("sub")
    device = box_index * sub_count + sub_index
    src_count = box_weights.shape[0]
    tgt_count = box_weights.shape[1]
    vec_len = box_weights.shape[2]
    current = box_weights
    bit_idx = 0
    level_idx = bit_idx
    my_child = sub_index // 2**bit_idx % 2
    omegas = level_omegas(velocity, device, level_idx, tgt_count)
    own_term = own_part(current, omegas, my_child, level_idx)
    partner = swapped(current, "sub", bit_idx)
    current = far_part(own_term, partner, omegas, my_child, level_idx)
    spread = lax.all_to_all(current, "box", split_axis=1, concat_axis=0, tiled=True)
    block_width = tgt_count // box_count
    for bit_idx in range(box_bits):
        level_idx = sub_bits + bit_idx
        weights, coord_in, coord_out = level_tables(level_idx % 2)
        row_count = spread.shape[0]
        col_count = spread.shape[1]
        groups = 2 ** (bit_idx + 1)
        vel_table = velocity[: sub_count * groups * tgt_count].reshape(groups, sub_count, tgt_count)
        omegas = lax.dynamic_slice(
            vel_table, (0, sub_index, box_index * block_width), (groups, 1, block_width)
        )
        omegas = omegas.reshape(2, col_count)
        blocks = spread.reshape(row_count // (2 * src_count), 2, src_count, col_count, vec_len)
        merged = merge_blocks(blocks, omegas, weights, coord_in, coord_out)
        spread = merged.reshape(row_count // 2, 2 * col_count, vec_len)
        if level_idx == levels // 2 - 1:
            spread = apply_switch(spread, switch_kernel)
    current = lax.all_to_all(spread, "box", split_axis=1, concat_axis=1, tiled=True)
    return current


def solution(mesh):
    return jax.shard_map(
        body,
        mesh=mesh,
        in_specs=(P(("shot", "box", "sub"), None, None), P("shot"), P()),
        out_specs=P("shot", ("box", "sub"), None),
        check_vma=False,
    )
```

profile of v0, /device:TPU:0, one launch (start us, length us, event | category | flops | bytes accessed | tf_op | source)
XLA Modules:
  0.0 46.1 jit_solution(10633600639100690880)
XLA Ops:
  0.0 0.5 %collective-permute-start = (f32[2,256,128]{2,1,0:T(8,128)}, f32[2,256,128]{2,1,0:T(8,128)S(1)}, u32[]{:S(2)}, u32[]{:S(2)}) collective-permute-start(f32[2,256,128]{2,1,0:T(8,128)} %param.3), channel_id=1, source_target_pairs={{0,1},{1,0},{2,3},{3,2},{4,5},{5,4},{6,7},{7,6},{8,9},{9,8},{10,11... | collective-permute-start | bytes 786440 | tf_op jit(solution)/shard_map/ppermute | solution.py:13
  0.7 0.7 %copy-done.2 = f32[4096]{0:T(1024)S(1)} copy-done((f32[4096]{0:T(1024)S(1)}, f32[4096]{0:T(1024)}, u32[]{:S(2)}) %copy-start.2) | copy-done | bytes 16408
  1.8 0.2 select_reduce_fusion.2
  2.0 0.3 select_reduce_fusion.1
  2.3 0.1 broadcast_multiply_fusion
  2.5 0.1 mul.1285
  2.6 0.1 mul.1290
  2.8 0.1 mul.1344
  2.9 0.1 mul.1350
  3.2 0.5 %slice-done.1 = f32[2048]{0:T(1024)S(1)} async-done(((f32[4096]{0:T(1024)}), f32[2048]{0:T(1024)S(1)}, s32[]{:S(2)}) %slice-start.1) | async-done | bytes 8216 | tf_op jit(solution)/shard_map/slice | solution.py:155
  3.9 0.3 multiply_cosine_fusion.5
  4.2 0.3 multiply_cosine_fusion.8
  4.6 0.4 slice-done
  5.2 0.3 broadcast_select_fusion
  5.5 0.1 mul.1347
  5.7 0.1 mul.1353
  5.9 0.5 %multiply_cosine_fusion.7 = (f32[2,64,64]{2,1,0:T(8,128)S(1)}, f32[2,64,64]{2,1,0:T(8,128)S(1)}, f32[2,64,64]{2,1,0:T(8,128)S(1)}, f32[2,64,64]{2,1,0:T(8,128)S(1)}) fusion(f32[64]{0:T(128)S(1)} %squeeze_stack_reshape.16, f32[2,64]{1,0:T(2,128)S(1)} %neg.34, f32[64]{0:T(128)S(1)} %squeeze_stack_reshape.17), kind=kLoop, calls=%fused_computation.103 | loop fusion | flops 16384 | bytes 132096 | tf_op jit(solution)/shard_map/cos | solution.py:59
  6.6 1.0 %multiply_cosine_fusion.2 = (f32[256,64]{1,0:T(8,128)S(1)}, f32[256,64]{1,0:T(8,128)S(1)}, f32[256,64]{1,0:T(8,128)S(1)}, f32[256,64]{1,0:T(8,128)S(1)}) fusion(f32[64]{0:T(128)S(1)} %get-tuple-element.97, f32[256]{0:T(256)S(1)} %get-tuple-element.7, f32[64]{0:T(128)S(1)} %get-tuple-element.98), kind=kLoop, calls=%fused_computation.59 | loop fusion | flops 32768 | bytes 263680 | tf_op jit(solution)/shard_map/cos | solution.py:59
  7.6 0.2 multiply_subtract_fusion.9
  7.8 0.1 pad_maximum_fusion
  7.9 0.3 multiply_cosine_fusion.4
  8.2 0.3 multiply_cosine_fusion.11
  8.6 0.1 select_n.114
  8.7 0.1 select_n.117
  8.8 0.1 mul.1391
  8.9 0.1 mul.1392
  9.1 0.4 fusion.39
  9.5 0.2 multiply_subtract_fusion.8
  9.6 0.1 pad_maximum_fusion.1
  9.8 0.4 convolution_add_fusion
  10.1 0.1 fusion.38
  10.3 0.1 copy.42
  10.6 0.8 %copy.29 = f32[2,256,128]{2,0,1:T(2,128)} copy(f32[2,256,128]{1,2,0:T(8,128)S(1)} %maximum_multiply_fusion) | data formatting | bytes 524288 | tf_op jit(solution)/shard_map/mul | solution.py:124
  11.4 6.8 %all-to-all-start = ((f32[2,256,128]{2,0,1:T(2,128)}), f32[2,256,128]{2,0,1:T(2,128)S(1)}, u32[]{:S(2)}, u32[]{:S(2)}) async-start(f32[2,256,128]{2,0,1:T(2,128)} %copy.29), calls=%async_computation | async-start | bytes 524288 | tf_op jit(solution)/shard_map/all_to_all | solution.py:147
  18.2 0.2 multiply_cosine_fusion.9
  18.4 1.0 %multiply_cosine_fusion.1 = (f32[2,128,64]{2,1,0:T(8,128)S(1)}, f32[2,128,64]{2,1,0:T(8,128)S(1)}, f32[2,128,64]{2,1,0:T(8,128)S(1)}, f32[2,128,64]{2,1,0:T(8,128)S(1)}) fusion(f32[64]{0:T(128)S(1)} %mul.1317, f32[2,128]{1,0:T(2,128)S(1)} %neg.35, f32[64]{0:T(128)S(1)} %mul.1330), kind=kLoop, calls=%fused_computation.57 | loop fusion | flops 32768 | bytes 263680 | tf_op jit(solution)/shard_map/cos | solution.py:59
  19.4 8.4 %all-to-all-done = f32[2,256,128]{2,0,1:T(2,128)S(1)} async-done(((f32[2,256,128]{2,0,1:T(2,128)}), f32[2,256,128]{2,0,1:T(2,128)S(1)}, u32[]{:S(2)}, u32[]{:S(2)}) %all-to-all-start) | async-done | bytes 262176 | tf_op jit(solution)/shard_map/all_to_all | solution.py:147
  28.3 0.7 %fusion = f32[4,2,2,32,128]{4,3,2,1,0:T(8,128)S(1)} fusion(f32[4,2,2,32,64]{4,3,2,1,0:T(8,128)S(1)} %get-tuple-element.32, f32[4,2,2,32,64]{4,3,2,1,0:T(8,128)S(1)} %get-tuple-element.31, f32[4,2,2,32,64]{4,3,2,1,0:T(8,128)S(1)} %get-tuple-element.30, f32[4,2,2,32,64]{4,3,2,1,0:T(8,128)S(1)} %get-tuple-element.29, ...), kind=kOutput, calls=%fused_computation.2 | convolution fusion | flops 201719808 | bytes 917504 | tf_op jit(solution)/shard_map/dot_general | solution.py:72
  28.9 0.2 multiply_subtract_fusion.5
  29.1 0.4 fusion.22
  29.9 0.7 %fusion.8 = f32[2,2,2,64,128]{4,3,2,1,0:T(8,128)S(1)} fusion(f32[2,2,2,64,64]{4,3,2,1,0:T(8,128)S(1)} %get-tuple-element.24, f32[2,2,2,64,64]{4,3,2,1,0:T(8,128)S(1)} %get-tuple-element.23, f32[2,2,2,64,64]{4,3,2,1,0:T(8,128)S(1)} %get-tuple-element.22, f32[2,2,2,64,64]{4,3,2,1,0:T(8,128)S(1)} %get-tuple-element.21, f32[128,128]{1,0:T(8,128)S(1)} %mul.1392, ...), kind=kOutput, calls=%fused_computation.10 | convolution fusion | flops 201752576 | bytes 917504 | tf_op jit(solution)/shard_map/dot_general | solution.py:72
  30.6 0.2 multiply_subtract_fusion.2
  30.8 0.1 maximum_multiply_fusion.3
  31.1 0.1 multiply_subtract_fusion
  31.3 0.9 %convolution_bitcast_fusion = f32[1,2,2,128,128]{3,4,2,1,0:T(8,128)S(1)} fusion(f32[1,2,2,128,64]{4,3,2,1,0:T(8,128)S(1)} %get-tuple-element.12, f32[1,2,2,128,64]{4,3,2,1,0:T(8,128)S(1)} %get-tuple-element.11, f32[1,2,2,128,64]{4,3,2,1,0:T(8,128)S(1)} %get-tuple-element.104, f32[1,2,2,128,64]{4,3,2,1,0:T(8,128)S(1)} %get-tuple-element.105, ...), kind=kOutput, calls=%fused_computation | convolution fusion | flops 201719808 | bytes 917504 | tf_op jit(solution)/shard_map/dot_general | solution.py:72
  32.7 0.1 copy.35
  32.8 12.5 %all_to_all.20 = f32[2,256,128]{2,0,1:T(2,128)S(1)} all-to-all(f32[2,256,128]{2,0,1:T(2,128)S(1)} %copy.35), channel_id=1, replica_groups=mesh['shot'=2,'box'=8,'sub'=2] {'box'}, dimensions={1} | all-to-all | bytes 524288 | tf_op jit(solution)/shard_map/all_to_all | solution.py:165
  45.3 0.7 %copy.36 = f32[2,256,128]{2,1,0:T(8,128)} copy(f32[2,256,128]{2,0,1:T(2,128)S(1)} %all_to_all.20) | data formatting | bytes 524288 | tf_op jit(solution)/shard_map/all_to_all | solution.py:165
  (66 shorter events, 3.1 us)
Async XLA Ops:
  0.0 29.1 %copy-start = (f32[128,128]{1,0:T(8,128)S(1)}, f32[128,128]{1,0:T(8,128)}, u32[]{:S(2)}) copy-start(f32[128,128]{1,0:T(8,128)} %param.5) | copy-start | bytes 196612
  0.0 9.4 %collective-permute-start = (f32[2,256,128]{2,1,0:T(8,128)}, f32[2,256,128]{2,1,0:T(8,128)S(1)}, u32[]{:S(2)}, u32[]{:S(2)}) collective-permute-start(f32[2,256,128]{2,1,0:T(8,128)} %param.3), channel_id=1, source_target_pairs={{0,1},{1,0},{2,3},{3,2},{4,5},{5,4},{6,7},{7,6},{8,9},{9,8},{10,11... | collective-permute-start | bytes 786440 | tf_op jit(solution)/shard_map/ppermute | solution.py:13
  0.7 0.7 %copy-start.2 = (f32[4096]{0:T(1024)S(1)}, f32[4096]{0:T(1024)}, u32[]{:S(2)}) copy-start(f32[4096]{0:T(1024)} %param.4) | copy-start | bytes 49156
  3.0 0.7 %slice-start.1 = ((f32[4096]{0:T(1024)}), f32[2048]{0:T(1024)S(1)}, s32[]{:S(2)}) async-start(f32[4096]{0:T(1024)} %param.4), calls=%async_computation.3 | async-start | bytes 16384 | tf_op jit(solution)/shard_map/slice | solution.py:155
  4.2 0.7 %slice-start = ((f32[4096]{0:T(1024)}), f32[1024]{0:T(1024)S(1)}, s32[]{:S(2)}) async-start(f32[4096]{0:T(1024)} %param.4), calls=%async_computation.2 | async-start | bytes 8192 | tf_op jit(solution)/shard_map/slice | solution.py:155
  6.6 1.0 %copy-start.1 = (f32[2,256,128]{2,1,0:T(8,128)S(1)}, f32[2,256,128]{2,1,0:T(8,128)}, u32[]{:S(2)}) copy-start(f32[2,256,128]{2,1,0:T(8,128)} %param.3) | copy-start | bytes 786436
  11.4 16.4 %all-to-all-start = ((f32[2,256,128]{2,0,1:T(2,128)}), f32[2,256,128]{2,0,1:T(2,128)S(1)}, u32[]{:S(2)}, u32[]{:S(2)}) async-start(f32[2,256,128]{2,0,1:T(2,128)} %copy.29), calls=%async_computation | async-start | bytes 524288 | tf_op jit(solution)/shard_map/all_to_all | solution.py:147
where the time goes:
time: 46.4 us; the launch traced here: 46.1 us
  blocking collectives  12.5 us (27%)
  waiting for transfers between devices  8.38 us (18%)
  starting transfers between devices  7.3 us (16%)
  local copies, waits for them, and re-layouts  7.19 us (15%)
  other arithmetic  6.78 us (15%)
  matrix products  3.37 us (7%)
  between operations  0.55 us (1%)
    all_to_all x1, blocking collectives, body(): lax.all_to_all(spread, 'box', split_axis=1, concat_axis=1, tiled=True)  12.5 us
    all_to_all x1, waiting for transfers between devices, body(): lax.all_to_all(current, 'box', split_axis=1, concat_axis=0, tiled=True)  8.38 us
    all_to_all x1, starting transfers between devices, body(): lax.all_to_all(current, 'box', split_axis=1, concat_axis=0, tiled=True)  6.81 us
    cos x8, other arithmetic, rotate(): cosines = jnp.cos(angles)  3.91 us
    dot_general x3, matrix products, merge_blocks(): jnp.dot(joined.reshape(-1, 4 * CHEB * CHEB), weights, precision=lax.Preci...  2.23 us
    sub x11, other arithmetic, rotate(): real_part * cosines - imag_part * sine_vals  1.13 us
    unnamed x9, local copies, waits for them, and re-layouts  0.93 us
    slice x6, local copies, waits for them, and re-layouts, body(): velocity[:sub_count * groups * tgt_count]  0.93 us
  transfers between devices with their start and end apart: 2, of which 1 were waited for; matrix products, arithmetic and copies ran while one was open for 18% of the time, Pallas kernels for 0%

commit v1 on v0

--- a/solution.py
+++ b/solution.py
@@ -144,7 +144,19 @@
     own_term = own_part(current, omegas, my_child, level_idx)
     partner = swapped(current, "sub", bit_idx)
     current = far_part(own_term, partner, omegas, my_child, level_idx)
-    spread = lax.all_to_all(current, "box", split_axis=1, concat_axis=0, tiled=True)
+    ways, here = (lax.axis_size("box"), lax.axis_index("box"))
+    width = current.shape[1] // ways
+    lengths = list(current.shape)
+    lengths[1] = width
+    height = lengths[0]
+    lengths[0] = height * ways
+    full = jnp.zeros(lengths, current.dtype)
+    for mask_2 in range(ways):
+        part = lax.dynamic_slice_in_dim(current, (here ^ mask_2) * width, width, axis=1)
+        if mask_2:
+            part = lax.ppermute(part, "box", [(d, d ^ mask_2) for d in range(ways)])
+        full = lax.dynamic_update_slice_in_dim(full, part, (here ^ mask_2) * height, axis=0)
+    spread = full
     block_width = tgt_count // box_count
     for bit_idx in range(box_bits):
         level_idx = sub_bits + bit_idx

time: 46.4 us -> 48.3 us (1.041)
  starting transfers between devices: 7.3 us -> 12.6 us
  blocking collectives: 12.5 us -> 10.6 us
  waiting for transfers between devices: 8.38 us -> 6.53 us
  other arithmetic: 6.78 us -> 7.35 us
  local copies, waits for them, and re-layouts: 7.19 us -> 6.66 us
    ppermute x0 -> x7, starting transfers between devices: none -> 12.1 us  [body(): part = lax.ppermute(part, 'box', [(d, d ^ mask_2) for d in range(ways)])]
    all_to_all x1 -> x0, waiting for transfers between devices: 8.38 us -> none  [body(): lax.all_to_all(current, 'box', split_axis=1, concat_axis=0, tiled=True)]
    all_to_all x1 -> x0, starting transfers between devices: 6.81 us -> none  [body(): lax.all_to_all(current, 'box', split_axis=1, concat_axis=0, tiled=True)]
    ppermute x0 -> x7, waiting for transfers between devices: none -> 6.52 us  [body(): part = lax.ppermute(part, 'box', [(d, d ^ mask_2) for d in range(ways)])]
    all_to_all x1, blocking collectives: 12.5 us -> 10.6 us  [body(): lax.all_to_all(spread, 'box', split_axis=1, concat_axis=1, tiled=True)]
    mul x1 -> x0, local copies, waits for them, and re-layouts: 0.84 us -> none  [far_part(): rotate(mixture, omegas[None, :, None] * coord_out[None, None, :])]
  transfers between devices with their start and end apart: 2 -> 8, of which waited for: 1 -> 3; matrix products, arithmetic and copies ran while one was open for 18% -> 18% of each run, Pallas kernels for 0% -> 0%
where the time goes in v1:
time: 48.3 us; the launch traced here: 47.8 us
  starting transfers between devices  12.6 us (26%)
  blocking collectives  10.6 us (22%)
  other arithmetic  7.35 us (15%)
  local copies, waits for them, and re-layouts  6.66 us (14%)
  waiting for transfers between devices  6.53 us (14%)
  matrix products  3.36 us (7%)
  between operations  0.65 us (1%)
    ppermute x7, starting transfers between devices, body(): part = lax.ppermute(part, 'box', [(d, d ^ mask_2) for d in range(ways)])  12.1 us
    all_to_all x1, blocking collectives, body(): lax.all_to_all(spread, 'box', split_axis=1, concat_axis=1, tiled=True)  10.6 us
    ppermute x7, waiting for transfers between devices, body(): part = lax.ppermute(part, 'box', [(d, d ^ mask_2) for d in range(ways)])  6.52 us
    cos x8, other arithmetic, rotate(): cosines = jnp.cos(angles)  4.14 us
    dot_general x3, matrix products, merge_blocks(): jnp.dot(joined.reshape(-1, 4 * CHEB * CHEB), weights, precision=lax.Preci...  2.22 us
    sub x11, other arithmetic, rotate(): real_part * cosines - imag_part * sine_vals  1.25 us
    slice x6, local copies, waits for them, and re-layouts, body(): velocity[:sub_count * groups * tgt_count]  1.24 us
    unnamed x9, local copies, waits for them, and re-layouts  1.1 us
  transfers between devices with their start and end apart: 8, of which 3 were waited for; matrix products, arithmetic and copies ran while one was open for 18% of the time, Pallas kernels for 0%

profile of v1, /device:TPU:0, one launch (start us, length us, event | category | flops | bytes accessed | tf_op | source)
XLA Modules:
  0.0 47.8 jit_solution(765300880222788616)
XLA Ops:
  0.0 0.5 %collective-permute-start = (f32[2,256,128]{2,1,0:T(8,128)}, f32[2,256,128]{2,1,0:T(8,128)S(1)}, u32[]{:S(2)}, u32[]{:S(2)}) collective-permute-start(f32[2,256,128]{2,1,0:T(8,128)} %param.3), channel_id=1, source_target_pairs={{0,1},{1,0},{2,3},{3,2},{4,5},{5,4},{6,7},{7,6},{8,9},{9,8},{10,11... | collective-permute-start | bytes 786440 | tf_op jit(solution)/shard_map/ppermute | solution.py:13
  0.7 0.7 %copy-done.2 = f32[4096]{0:T(1024)S(1)} copy-done((f32[4096]{0:T(1024)S(1)}, f32[4096]{0:T(1024)}, u32[]{:S(2)}) %copy-start.2) | copy-done | bytes 16408
  1.4 0.7 %slice-done = f32[1024]{0:T(1024)S(1)} async-done(((f32[4096]{0:T(1024)}), f32[1024]{0:T(1024)S(1)}, s32[]{:S(2)}) %slice-start) | async-done | bytes 4120 | tf_op jit(solution)/shard_map/slice | solution.py:167
  2.3 0.2 multiply_cosine_fusion.9
  2.7 0.3 multiply_cosine_fusion.5
  3.0 0.4 copy-done.3
  3.6 0.2 select_reduce_fusion.2
  3.9 0.3 select_reduce_fusion.1
  4.3 0.1 broadcast_multiply_fusion
  5.1 0.5 %slice-done.1 = f32[2048]{0:T(1024)S(1)} async-done(((f32[4096]{0:T(1024)}), f32[2048]{0:T(1024)S(1)}, s32[]{:S(2)}) %slice-start.1) | async-done | bytes 8216 | tf_op jit(solution)/shard_map/slice | solution.py:167
  5.9 0.3 multiply_cosine_fusion.6
  6.2 0.5 %multiply_cosine_fusion.2 = (f32[256,64]{1,0:T(8,128)S(1)}, f32[256,64]{1,0:T(8,128)S(1)}) fusion(f32[64]{0:T(128)S(1)} %mul.1346, f32[256]{0:T(256)S(1)} %get-tuple-element.8), kind=kLoop, calls=%fused_computation.61 | loop fusion | flops 16384 | bytes 132352 | tf_op jit(solution)/shard_map/cos | solution.py:59
  6.9 0.3 broadcast_select_fusion
  7.2 0.1 mul.1405
  7.4 0.5 %multiply_cosine_fusion.8 = (f32[2,64,64]{2,1,0:T(8,128)S(1)}, f32[2,64,64]{2,1,0:T(8,128)S(1)}, f32[2,64,64]{2,1,0:T(8,128)S(1)}, f32[2,64,64]{2,1,0:T(8,128)S(1)}) fusion(f32[64]{0:T(128)S(1)} %squeeze_stack_reshape.16, f32[2,64]{1,0:T(2,128)S(1)} %neg.34, f32[64]{0:T(128)S(1)} %squeeze_stack_reshape.17), kind=kLoop, calls=%fused_computation.105 | loop fusion | flops 16384 | bytes 132096 | tf_op jit(solution)/shard_map/cos | solution.py:59
  7.9 0.3 multiply_cosine_fusion.11
  8.2 1.0 %multiply_cosine_fusion.1 = (f32[2,128,64]{2,1,0:T(8,128)S(1)}, f32[2,128,64]{2,1,0:T(8,128)S(1)}, f32[2,128,64]{2,1,0:T(8,128)S(1)}, f32[2,128,64]{2,1,0:T(8,128)S(1)}) fusion(f32[64]{0:T(128)S(1)} %mul.1375, f32[2,128]{1,0:T(2,128)S(1)} %neg.35, f32[64]{0:T(128)S(1)} %mul.1388), kind=kLoop, calls=%fused_computation.59 | loop fusion | flops 32768 | bytes 263680 | tf_op jit(solution)/shard_map/cos | solution.py:59
  9.2 1.0 %multiply_cosine_fusion.3 = (f32[256,64]{1,0:T(8,128)S(1)}, f32[256,64]{1,0:T(8,128)S(1)}, f32[256,64]{1,0:T(8,128)S(1)}, f32[256,64]{1,0:T(8,128)S(1)}) fusion(f32[64]{0:T(128)S(1)} %get-tuple-element.103, f32[256]{0:T(256)S(1)} %get-tuple-element.7, f32[64]{0:T(128)S(1)} %get-tuple-element.104), kind=kLoop, calls=%fused_computation.63 | loop fusion | flops 32768 | bytes 263680 | tf_op jit(solution)/shard_map/cos | solution.py:59
  10.2 0.2 multiply_subtract_fusion.10
  10.4 0.1 pad_maximum_fusion
  10.6 0.1 select_n.160
  11.0 0.4 fusion.40
  11.4 0.2 multiply_subtract_fusion.9
  11.5 0.1 pad_maximum_fusion.1
  11.7 0.4 convolution_add_fusion
  12.1 0.2 multiply_subtract_fusion.8
  12.2 0.1 maximum_multiply_fusion
  12.4 2.6 %collective-permute-start.1 = (f32[2,32,128]{2,1,0:T(8,128)S(1)}, f32[2,32,128]{2,1,0:T(8,128)S(1)}, u32[]{:S(2)}, u32[]{:S(2)}) collective-permute-start(f32[2,32,128]{2,1,0:T(8,128)S(1)} %get-tuple-element.45), channel_id=1, source_target_pairs={{0,2},{2,0},{4,6},{6,4},{8,10},{10,8},{12,14},{14,12},{1,3},{3,1},... | collective-permute-start | bytes 98312 | tf_op jit(solution)/shard_map/ppermute | solution.py:157
  15.0 0.1 mul.1449
  15.3 1.6 %collective-permute-start.2 = (f32[2,32,128]{2,1,0:T(8,128)S(1)}, f32[2,32,128]{2,1,0:T(8,128)S(1)}, u32[]{:S(2)}, u32[]{:S(2)}) collective-permute-start(f32[2,32,128]{2,1,0:T(8,128)S(1)} %get-tuple-element.44), channel_id=1, source_target_pairs={{0,4},{2,6},{4,0},{6,2},{8,12},{10,14},{12,8},{14,10},{1,5},{3,7},... | collective-permute-start | bytes 98312 | tf_op jit(solution)/shard_map/ppermute | solution.py:157
  17.0 3.0 %collective-permute-start.4 = (f32[2,32,128]{2,1,0:T(8,128)S(1)}, f32[2,32,128]{2,1,0:T(8,128)S(1)}, u32[]{:S(2)}, u32[]{:S(2)}) collective-permute-start(f32[2,32,128]{2,1,0:T(8,128)S(1)} %get-tuple-element.42), channel_id=1, source_target_pairs={{0,8},{2,10},{4,12},{6,14},{8,0},{10,2},{12,4},{14,6},{1,9},{3,11}... | collective-permute-start | bytes 98312 | tf_op jit(solution)/shard_map/ppermute | solution.py:157
  19.9 1.3 %collective-permute-start.5 = (f32[2,32,128]{2,1,0:T(8,128)S(1)}, f32[2,32,128]{2,1,0:T(8,128)S(1)}, u32[]{:S(2)}, u32[]{:S(2)}) collective-permute-start(f32[2,32,128]{2,1,0:T(8,128)S(1)} %get-tuple-element.41), channel_id=1, source_target_pairs={{0,10},{2,8},{4,14},{6,12},{8,2},{10,0},{12,6},{14,4},{1,11},{3,9}... | collective-permute-start | bytes 98312 | tf_op jit(solution)/shard_map/ppermute | solution.py:157
  21.2 3.6 %collective-permute-start.6 = (f32[2,32,128]{2,1,0:T(8,128)S(1)}, f32[2,32,128]{2,1,0:T(8,128)S(1)}, u32[]{:S(2)}, u32[]{:S(2)}) collective-permute-start(f32[2,32,128]{2,1,0:T(8,128)S(1)} %get-tuple-element.40), channel_id=1, source_target_pairs={{0,12},{2,14},{4,8},{6,10},{8,4},{10,6},{12,0},{14,2},{1,13},{3,15... | collective-permute-start | bytes 98312 | tf_op jit(solution)/shard_map/ppermute | solution.py:157
  25.0 0.8 %collective-permute-done.5 = f32[2,32,128]{2,1,0:T(8,128)S(1)} collective-permute-done((f32[2,32,128]{2,1,0:T(8,128)S(1)}, f32[2,32,128]{2,1,0:T(8,128)S(1)}, u32[]{:S(2)}, u32[]{:S(2)}) %collective-permute-start.5) | collective-permute-done | bytes 32800 | tf_op jit(solution)/shard_map/ppermute | solution.py:157
  25.8 1.3 %collective-permute-done.6 = f32[2,32,128]{2,1,0:T(8,128)S(1)} collective-permute-done((f32[2,32,128]{2,1,0:T(8,128)S(1)}, f32[2,32,128]{2,1,0:T(8,128)S(1)}, u32[]{:S(2)}, u32[]{:S(2)}) %collective-permute-start.6) | collective-permute-done | bytes 32800 | tf_op jit(solution)/shard_map/ppermute | solution.py:157
  27.1 4.3 %collective-permute-done.7 = f32[2,32,128]{2,1,0:T(8,128)S(1)} collective-permute-done((f32[2,32,128]{2,1,0:T(8,128)S(1)}, f32[2,32,128]{2,1,0:T(8,128)S(1)}, u32[]{:S(2)}, u32[]{:S(2)}) %collective-permute-start.7) | collective-permute-done | bytes 32800 | tf_op jit(solution)/shard_map/ppermute | solution.py:157
  31.9 0.7 %fusion = f32[4,2,2,32,128]{4,3,2,1,0:T(8,128)S(1)} fusion(f32[4,2,2,32,64]{4,3,2,1,0:T(8,128)S(1)} %get-tuple-element.32, f32[4,2,2,32,64]{4,3,2,1,0:T(8,128)S(1)} %get-tuple-element.31, f32[4,2,2,32,64]{4,3,2,1,0:T(8,128)S(1)} %get-tuple-element.30, f32[4,2,2,32,64]{4,3,2,1,0:T(8,128)S(1)} %get-tuple-element.29, ...), kind=kOutput, calls=%fused_computation.2 | convolution fusion | flops 201719808 | bytes 917504 | tf_op jit(solution)/shard_map/dot_general | solution.py:72
  32.6 0.2 multiply_subtract_fusion.5
  32.7 0.4 fusion.22
  33.6 0.7 %fusion.8 = f32[2,2,2,64,128]{4,3,2,1,0:T(8,128)S(1)} fusion(f32[2,2,2,64,64]{4,3,2,1,0:T(8,128)S(1)} %get-tuple-element.26, f32[2,2,2,64,64]{4,3,2,1,0:T(8,128)S(1)} %get-tuple-element.25, f32[2,2,2,64,64]{4,3,2,1,0:T(8,128)S(1)} %get-tuple-element.24, f32[2,2,2,64,64]{4,3,2,1,0:T(8,128)S(1)} %get-tuple-element.23, f32[128,128]{1,0:T(8,128)S(1)} %mul.1450, ...), kind=kOutput, calls=%fused_computation.10 | convolution fusion | flops 201752576 | bytes 917504 | tf_op jit(solution)/shard_map/dot_general | solution.py:72
  34.2 0.2 multiply_subtract_fusion.2
  34.4 0.1 maximum_multiply_fusion.3
  34.8 0.1 multiply_subtract_fusion
  34.9 0.9 %convolution_bitcast_fusion = f32[1,2,2,128,128]{3,4,2,1,0:T(8,128)S(1)} fusion(f32[1,2,2,128,64]{4,3,2,1,0:T(8,128)S(1)} %get-tuple-element.12, f32[1,2,2,128,64]{4,3,2,1,0:T(8,128)S(1)} %get-tuple-element.11, f32[1,2,2,128,64]{4,3,2,1,0:T(8,128)S(1)} %get-tuple-element.110, f32[1,2,2,128,64]{4,3,2,1,0:T(8,128)S(1)} %get-tuple-element.111, ...), kind=kOutput, calls=%fused_computation | convolution fusion | flops 201719808 | bytes 917504 | tf_op jit(solution)/shard_map/dot_general | solution.py:72
  36.1 0.1 maximum_multiply_fusion.4
  36.3 0.2 copy.22
  36.5 10.6 %all_to_all.5 = f32[2,256,128]{2,0,1:T(2,128)S(1)} all-to-all(f32[2,256,128]{2,0,1:T(2,128)S(1)} %copy.22), channel_id=1, replica_groups=mesh['shot'=2,'box'=8,'sub'=2] {'box'}, dimensions={1} | all-to-all | bytes 524288 | tf_op jit(solution)/shard_map/all_to_all | solution.py:177
  47.1 0.7 %copy.23 = f32[2,256,128]{2,1,0:T(8,128)} copy(f32[2,256,128]{2,0,1:T(2,128)S(1)} %all_to_all.5) | data formatting | bytes 524288 | tf_op jit(solution)/shard_map/all_to_all | solution.py:177
  (81 shorter events, 3.8 us)
Async XLA Ops:
  0.0 32.7 %copy-start = (f32[128,128]{1,0:T(8,128)S(1)}, f32[128,128]{1,0:T(8,128)}, u32[]{:S(2)}) copy-start(f32[128,128]{1,0:T(8,128)} %param.5) | copy-start | bytes 196612
  0.0 11.4 %collective-permute-start = (f32[2,256,128]{2,1,0:T(8,128)}, f32[2,256,128]{2,1,0:T(8,128)S(1)}, u32[]{:S(2)}, u32[]{:S(2)}) collective-permute-start(f32[2,256,128]{2,1,0:T(8,128)} %param.3), channel_id=1, source_target_pairs={{0,1},{1,0},{2,3},{3,2},{4,5},{5,4},{6,7},{7,6},{8,9},{9,8},{10,11... | collective-permute-start | bytes 786440 | tf_op jit(solution)/shard_map/ppermute | solution.py:13
  0.7 0.7 %copy-start.2 = (f32[4096]{0:T(1024)S(1)}, f32[4096]{0:T(1024)}, u32[]{:S(2)}) copy-start(f32[4096]{0:T(1024)} %param.4) | copy-start | bytes 49156
  1.4 0.7 %slice-start = ((f32[4096]{0:T(1024)}), f32[1024]{0:T(1024)S(1)}, s32[]{:S(2)}) async-start(f32[4096]{0:T(1024)} %param.4), calls=%async_computation.1 | async-start | bytes 8192 | tf_op jit(solution)/shard_map/slice | solution.py:167
  2.7 0.7 %copy-start.3 = (f32[4096]{0:T(1024)S(1)}, f32[4096]{0:T(1024)}, u32[]{:S(2)}) copy-start(f32[4096]{0:T(1024)} %param.4) | copy-start | bytes 49156
  5.0 0.7 %slice-start.1 = ((f32[4096]{0:T(1024)}), f32[2048]{0:T(1024)S(1)}, s32[]{:S(2)}) async-start(f32[4096]{0:T(1024)} %param.4), calls=%async_computation.2 | async-start | bytes 16384 | tf_op jit(solution)/shard_map/slice | solution.py:167
  9.2 1.0 %copy-start.1 = (f32[2,256,128]{2,1,0:T(8,128)S(1)}, f32[2,256,128]{2,1,0:T(8,128)}, u32[]{:S(2)}) copy-start(f32[2,256,128]{2,1,0:T(8,128)} %param.3) | copy-start | bytes 786436
  12.4 8.8 %collective-permute-start.1 = (f32[2,32,128]{2,1,0:T(8,128)S(1)}, f32[2,32,128]{2,1,0:T(8,128)S(1)}, u32[]{:S(2)}, u32[]{:S(2)}) collective-permute-start(f32[2,32,128]{2,1,0:T(8,128)S(1)} %get-tuple-element.45), channel_id=1, source_target_pairs={{0,2},{2,0},{4,6},{6,4},{8,10},{10,8},{12,14},{14,12},{1,3},{3,1},... | collective-permute-start | bytes 98312 | tf_op jit(solution)/shard_map/ppermute | solution.py:157
  15.3 9.5 %collective-permute-start.2 = (f32[2,32,128]{2,1,0:T(8,128)S(1)}, f32[2,32,128]{2,1,0:T(8,128)S(1)}, u32[]{:S(2)}, u32[]{:S(2)}) collective-permute-start(f32[2,32,128]{2,1,0:T(8,128)S(1)} %get-tuple-element.44), channel_id=1, source_target_pairs={{0,4},{2,6},{4,0},{6,2},{8,12},{10,14},{12,8},{14,10},{1,5},{3,7},... | collective-permute-start | bytes 98312 | tf_op jit(solution)/shard_map/ppermute | solution.py:157
  16.9 8.0 %collective-permute-start.3 = (f32[2,32,128]{2,1,0:T(8,128)S(1)}, f32[2,32,128]{2,1,0:T(8,128)S(1)}, u32[]{:S(2)}, u32[]{:S(2)}) collective-permute-start(f32[2,32,128]{2,1,0:T(8,128)S(1)} %get-tuple-element.43), channel_id=1, source_target_pairs={{0,6},{2,4},{4,2},{6,0},{8,14},{10,12},{12,10},{14,8},{1,7},{3,5},... | collective-permute-start | bytes 98312 | tf_op jit(solution)/shard_map/ppermute | solution.py:157
  17.0 8.0 %collective-permute-start.4 = (f32[2,32,128]{2,1,0:T(8,128)S(1)}, f32[2,32,128]{2,1,0:T(8,128)S(1)}, u32[]{:S(2)}, u32[]{:S(2)}) collective-permute-start(f32[2,32,128]{2,1,0:T(8,128)S(1)} %get-tuple-element.42), channel_id=1, source_target_pairs={{0,8},{2,10},{4,12},{6,14},{8,0},{10,2},{12,4},{14,6},{1,9},{3,11}... | collective-permute-start | bytes 98312 | tf_op jit(solution)/shard_map/ppermute | solution.py:157
  19.9 5.9 %collective-permute-start.5 = (f32[2,32,128]{2,1,0:T(8,128)S(1)}, f32[2,32,128]{2,1,0:T(8,128)S(1)}, u32[]{:S(2)}, u32[]{:S(2)}) collective-permute-start(f32[2,32,128]{2,1,0:T(8,128)S(1)} %get-tuple-element.41), channel_id=1, source_target_pairs={{0,10},{2,8},{4,14},{6,12},{8,2},{10,0},{12,6},{14,4},{1,11},{3,9}... | collective-permute-start | bytes 98312 | tf_op jit(solution)/shard_map/ppermute | solution.py:157
  21.2 5.9 %collective-permute-start.6 = (f32[2,32,128]{2,1,0:T(8,128)S(1)}, f32[2,32,128]{2,1,0:T(8,128)S(1)}, u32[]{:S(2)}, u32[]{:S(2)}) collective-permute-start(f32[2,32,128]{2,1,0:T(8,128)S(1)} %get-tuple-element.40), channel_id=1, source_target_pairs={{0,12},{2,14},{4,8},{6,10},{8,4},{10,6},{12,0},{14,2},{1,13},{3,15... | collective-permute-start | bytes 98312 | tf_op jit(solution)/shard_map/ppermute | solution.py:157
  24.8 6.7 %collective-permute-start.7 = (f32[2,32,128]{2,1,0:T(8,128)S(1)}, f32[2,32,128]{2,1,0:T(8,128)S(1)}, u32[]{:S(2)}, u32[]{:S(2)}) collective-permute-start(f32[2,32,128]{2,1,0:T(8,128)S(1)} %get-tuple-element.39), channel_id=1, source_target_pairs={{0,14},{2,12},{4,10},{6,8},{8,6},{10,4},{12,2},{14,0},{1,15},{3,13... | collective-permute-start | bytes 98312 | tf_op jit(solution)/shard_map/ppermute | solution.py:157
